TPU v7x, 256 devices: a whole 4x4x8 slice. The times are simulated.
256 devices in a mesh: expert: 64 (over x, z, core), dp: 4 (over y).
Axes of the slice: x: 4, y: 4, z: 8, core: 2. Of those that a mesh axis runs over, the one named last changes fastest.
Arguments:
- tokens: bfloat16 [8192, 3584], P('expert', 'dp'), may hold values from -6 to 6
- cotangent: bfloat16 [8192, 3584], P('expert', 'dp'), may hold values from -6 to 6
- expert_ids: int32 [8192, 8], P('expert'), may hold values from 0 to 63, all different within a row; in each aligned block of 128 rows (0 to 127, 128 to 255, ...) at most 18 rows name the same one
- gate_units: int32 [8192, 8], P('expert'), may hold values from 1 to 255
- w_in: bfloat16 [64, 3584, 1024], P('expert', 'dp'), may hold values from -0.09375 to 0.09375
- w_out: bfloat16 [64, 1024, 3584], P('expert', None, 'dp'), may hold values from -0.1875 to 0.1875
- shared_in: bfloat16 [3584, 1024], P('dp', 'expert'), may hold values from -0.09375 to 0.09375
- shared_out: bfloat16 [1024, 3584], P('expert', 'dp'), may hold values from -0.1875 to 0.1875
Outputs:
- mixed_out: bfloat16 [8192, 3584], P('expert', 'dp')
- input_grad: bfloat16 [8192, 3584], P('expert', 'dp')
- grad_w_in: bfloat16 [64, 3584, 1024], P('expert', 'dp')
- grad_w_out: bfloat16 [64, 1024, 3584], P('expert', None, 'dp')
- grad_shared_in: bfloat16 [3584, 1024], P('dp', 'expert')
- grad_shared_out: bfloat16 [1024, 3584], P('expert', 'dp')
Inputs may be any that keep to these rules, and one draw needn't show every extreme that they name: `expert_ids`: each row names 8 different experts. In each aligned block of 128 rows (the tokens of one index of expert) no expert is named by more than 18 rows, a bound that some block reaches.
All inputs are finite; a program needn't handle non-finite values.
Results may differ from a plain program's by a relative error of at most 0.02.
Values may be sent and summed in bfloat16 or wider, within the bound.
No kernel may reach another device: no remote copies, remote signals or barrier semaphores. Data moves between devices by JAX's collectives and lax.ppermute only.
A program may use at most 128 MiB of HBM per device.

v0:
```python
import jax
import jax.numpy as jnp
from jax import lax
from jax.sharding import PartitionSpec as P


def silu_slope(inputs):
    logistic = jax.nn.sigmoid(inputs)
    return logistic * (1.0 + inputs * (1.0 - logistic))


def contract(first_op, second_op, first_axis, second_axis):
    return lax.dot_general(
        first_op,
        second_op,
        (((first_axis,), (second_axis,)), ((), ())),
        preferred_element_type=jnp.float32,
    )


def local(tokens, cotangent, expert_ids, gate_units, w_in, w_out, shared_in, shared_out):
    experts = lax.axis_size("expert")
    tok_rows, features = tokens.shape
    per_token = expert_ids.shape[1]
    capacity = min(tok_rows, tok_rows * per_token // experts + tok_rows // 64)
    slot_count = experts * capacity
    pair_count = tok_rows * per_token
    flat_ids = expert_ids.reshape(pair_count)
    weights = gate_units.reshape(pair_count).astype(jnp.float32) / 256.0
    one_hot = (flat_ids[:, None] == jnp.arange(experts, dtype=jnp.int32)[None, :]).astype(jnp.int32)
    slot_rank = jnp.sum((jnp.cumsum(one_hot, axis=0) - 1) * one_hot, axis=1)
    target = flat_ids * capacity + slot_rank
    pair_of_slot = (
        jnp.zeros((slot_count,), jnp.int32).at[target].set(jnp.arange(pair_count, dtype=jnp.int32))
    )
    filled = jnp.zeros((slot_count,), jnp.bool_).at[target].set(True)
    token_of_slot = pair_of_slot // per_token
    outgoing = jnp.where(filled[:, None], tokens[token_of_slot], jnp.zeros((), jnp.bfloat16))
    arrived = lax.all_to_all(
        outgoing.reshape(experts, capacity, features),
        "expert",
        split_axis=0,
        concat_axis=0,
        tiled=True,
    ).reshape(slot_count, features)
    full_in, full_out = (
        lax.all_gather(shared_in, "expert", axis=1, tiled=True),
        lax.all_gather(shared_out, "expert", axis=0, tiled=True),
    )
    routed_part = jnp.dot(arrived, w_in[0], preferred_element_type=jnp.float32)
    shared_part = jnp.dot(tokens, full_in, preferred_element_type=jnp.float32)
    pre_act, shared_pre = (
        lax.psum(routed_part.astype(jnp.bfloat16), "dp").astype(jnp.float32),
        lax.psum(shared_part.astype(jnp.bfloat16), "dp").astype(jnp.float32),
    )
    hidden = jax.nn.silu(pre_act).astype(jnp.bfloat16)
    shared_hidden = jax.nn.silu(shared_pre).astype(jnp.bfloat16)
    expert_out = jnp.dot(hidden, w_out[0], preferred_element_type=jnp.float32).astype(jnp.bfloat16)
    returned = lax.all_to_all(
        expert_out.reshape(experts, capacity, features),
        "expert",
        split_axis=0,
        concat_axis=0,
        tiled=True,
    ).reshape(slot_count, features)
    picked = returned[target].astype(jnp.float32) * weights[:, None]
    routed_sum = jnp.sum(picked.reshape(tok_rows, per_token, features), axis=1)
    mixed_out = (
        jnp.dot(shared_hidden, full_out, preferred_element_type=jnp.float32) + routed_sum
    ).astype(jnp.bfloat16)
    scaled = weights[pair_of_slot][:, None] * cotangent[token_of_slot].astype(jnp.float32)
    grad_out = jnp.where(filled[:, None], scaled, jnp.float32(0.0)).astype(jnp.bfloat16)
    grad_rows = lax.all_to_all(
        grad_out.reshape(experts, capacity, features),
        "expert",
        split_axis=0,
        concat_axis=0,
        tiled=True,
    ).reshape(slot_count, features)
    routed_back = contract(grad_rows, w_out[0], 1, 1)
    shared_back = contract(cotangent, full_out, 1, 1)
    hidden_grad, shared_hgrad = (
        lax.psum(routed_back.astype(jnp.bfloat16), "dp").astype(jnp.float32),
        lax.psum(shared_back.astype(jnp.bfloat16), "dp").astype(jnp.float32),
    )
    pre_grad = (hidden_grad * silu_slope(pre_act)).astype(jnp.bfloat16)
    shared_pgrad = (shared_hgrad * silu_slope(shared_pre)).astype(jnp.bfloat16)
    input_rows = contract(pre_grad, w_in[0], 1, 1).astype(jnp.bfloat16)
    sent_back = lax.all_to_all(
        input_rows.reshape(experts, capacity, features),
        "expert",
        split_axis=0,
        concat_axis=0,
        tiled=True,
    ).reshape(slot_count, features)
    routed_dx = jnp.sum(
        sent_back[target].astype(jnp.float32).reshape(tok_rows, per_token, features), axis=1
    )
    input_grad = (contract(shared_pgrad, full_in, 1, 1) + routed_dx).astype(jnp.bfloat16)
    grad_w_in = contract(arrived, pre_grad, 0, 0).astype(jnp.bfloat16)[None]
    grad_w_out = contract(hidden, grad_rows, 0, 0).astype(jnp.bfloat16)[None]
    partial_in = contract(tokens, shared_pgrad, 0, 0)
    partial_out = contract(shared_hidden, cotangent, 0, 0)
    summed_in, summed_out = (
        lax.psum_scatter(partial_in, "expert", scatter_dimension=1, tiled=True),
        lax.psum_scatter(partial_out, "expert", scatter_dimension=0, tiled=True),
    )
    return (
        mixed_out,
        input_grad,
        grad_w_in,
        grad_w_out,
        summed_in.astype(jnp.bfloat16),
        summed_out.astype(jnp.bfloat16),
    )


def solution(mesh):
    return jax.shard_map(
        local,
        mesh=mesh,
        in_specs=(
            P("expert", "dp"),
            P("expert", "dp"),
            P("expert", None),
            P("expert", None),
            P("expert", "dp", None),
            P("expert", None, "dp"),
            P("dp", "expert"),
            P("expert", "dp"),
        ),
        out_specs=(
            P("expert", "dp"),
            P("expert", "dp"),
            P("expert", "dp", None),
            P("expert", None, "dp"),
            P("dp", "expert"),
            P("expert", "dp"),
        ),
        check_vma=False,
    )
```

profile of v0, /device:TPU:8, one launch (start us, length us, event | category | flops | bytes accessed | tf_op | source)
XLA Modules:
  0.0 643.2 jit_solution(7571708094391485513)
XLA Ops:
  7.2 0.7 all-gather.5.cloned.1.call-update
  7.9 0.7 broadcast_multiply_fusion
  8.6 0.8 copy.16
  9.4 0.1 eq.29
  9.6 0.1 copy.15
  9.7 0.1 mul.68
  9.8 18.0 %reduce-window.6 = s32[64,8,128]{2,1,0:T(8,128)S(1)} reduce-window(s32[64,8,128]{2,1,0:T(8,128)S(1)} %fusion.25, s32[]{:T(128)} %constant.19.clone.1), window={size=1x1x128 pad=0_0x0_0x127_0}, to_apply=%region_1.2 | reduce-window | flops 8323072 | bytes 524292 | tf_op jit(solution)/shard_map/reduce-window
  27.8 0.1 slice.18
  28.0 0.1 copy.18
  28.2 0.1 add_add_fusion
  28.5 4.3 scatter_custom_fusion.1
  32.8 4.3 scatter_custom_fusion
  37.2 0.1 broadcast_in_dim.54
  37.4 4.9 gather_fusion
  42.3 4.1 gather.18
  46.4 3.8 broadcast_select_fusion
  50.3 12.3 %all-to-all-start = ((bf16[64,18,896]{2,1,0:T(8,128)(2,1)}), bf16[64,18,896]{2,1,0:T(8,128)(2,1)}, u32[]{:S(2)}, u32[]{:S(2)}) async-start(bf16[64,18,896]{2,1,0:T(8,128)(2,1)} %broadcast_select_fusion), calls=%async_computation | async-start | bytes 5505024 | tf_op jit(solution)/shard_map/all_to_all | solution.py:39
  62.6 0.7 all-gather.3.cloned.1.call-update
  63.3 0.1 copy.20
  63.4 0.1 div.38
  63.5 4.6 gather_fusion.2
  68.1 0.1 mul.76
  68.3 4.9 gather_fusion.3
  73.2 4.6 reshape.130
  77.8 4.1 select_convert_fusion
  81.8 50.9 %all-to-all-done = bf16[64,18,896]{2,1,0:T(8,128)(2,1)} async-done(((bf16[64,18,896]{2,1,0:T(8,128)(2,1)}), bf16[64,18,896]{2,1,0:T(8,128)(2,1)}, u32[]{:S(2)}, u32[]{:S(2)}) %all-to-all-start) | async-done | bytes 2064416 | tf_op jit(solution)/shard_map/all_to_all | solution.py:39
  132.8 5.7 all-to-all-start.2
  138.5 0.2 all-reduce.3.cloned.1.call-start
  138.8 2.9 convolution_convert_fusion.4
  141.7 39.4 %all-gather.3.cloned.1.call-done = bf16[896,1024]{0,1:T(8,128)(2,1)} async-done(((bf16[896,16]{0,1:T(8,128)(2,1)}), bf16[896,1024]{0,1:T(8,128)(2,1)}) %all-gather.3.cloned.1.call-update) | async-done | bytes 1835024 | tf_op jit(solution)/shard_map/all_gather | solution.py:47
  181.1 2.9 convolution_convert_fusion.5
  184.0 4.2 reshape.123
  188.2 5.5 convolution_convert_fusion.1
  193.6 13.7 %all-to-all-done.2 = bf16[64,18,896]{2,1,0:T(8,128)(2,1)} async-done(((bf16[64,18,896]{2,1,0:T(8,128)(2,1)}), bf16[64,18,896]{2,1,0:T(8,128)(2,1)}, u32[]{:S(2)}, u32[]{:S(2)}) %all-to-all-start.2) | async-done | bytes 2064416 | tf_op jit(solution)/shard_map/all_to_all | solution.py:73
  207.4 4.1 reshape.126
  211.5 6.2 convolution_convert_fusion
  217.8 111.4 %all-reduce.3.cloned.1.call-done = (bf16[1152,1024]{1,0:T(8,128)(2,1)}, bf16[128,1024]{1,0:T(8,128)(2,1)}, bf16[1152,1024]{1,0:T(8,128)(2,1)}, bf16[128,1024]{1,0:T(8,128)(2,1)}) async-done(((bf16[1152,1024]{1,0:T(8,128)(2,1)}, bf16[128,1024]{1,0:T(8,128)(2,1)}, bf16[1152,1024]{1,0:T(8,128)(2,1)}, bf16[128,1024]{1,0:T(8,128)(2,1)}), (bf16[1152,1024]{1,0:T(8,128)(2,1)}, bf16[128,1024]{1,0:T(8,128)(2,1)}, ...) | async-done | bytes 5242896 | tf_op jit(solution)/shard_map/psum | solution.py:53
  329.2 3.6 convolution_bitcast_fusion
  332.8 4.3 fusion.7
  337.1 1.4 copy-done.6
  338.5 3.8 convolution_convert_fusion.2
  342.3 4.2 reshape.127
  346.5 10.8 %all-to-all-start.3 = ((bf16[64,18,896]{2,1,0:T(8,128)(2,1)}), bf16[64,18,896]{2,1,0:T(8,128)(2,1)}, u32[]{:S(2)}, u32[]{:S(2)}) async-start(bf16[64,18,896]{2,1,0:T(8,128)(2,1)} %reshape.127), calls=%async_computation.3 | async-start | bytes 5505024 | tf_op jit(solution)/shard_map/all_to_all | solution.py:89
  357.3 0.3 reduce-scatter.5.cloned.1.call-start
  357.6 2.5 fusion.32
  360.2 5.0 convolution_convert_fusion.3
  365.1 2.3 reshape.124
  367.5 56.1 %all-to-all-done.3 = bf16[64,18,896]{2,1,0:T(8,128)(2,1)} async-done(((bf16[64,18,896]{2,1,0:T(8,128)(2,1)}), bf16[64,18,896]{2,1,0:T(8,128)(2,1)}, u32[]{:S(2)}, u32[]{:S(2)}) %all-to-all-start.3) | async-done | bytes 2064416 | tf_op jit(solution)/shard_map/all_to_all | solution.py:89
  423.6 7.0 %all-to-all-start.1 = ((bf16[64,18,896]{2,1,0:T(8,128)(2,1)}), bf16[64,18,896]{2,1,0:T(8,128)(2,1)}, u32[]{:S(2)}, u32[]{:S(2)}) async-start(bf16[64,18,896]{2,1,0:T(8,128)(2,1)} %reshape.124), calls=%async_computation.1 | async-start | bytes 5505024 | tf_op jit(solution)/shard_map/all_to_all | solution.py:59
  430.6 5.6 convert_bitcast_fusion.1
  436.3 4.1 convert_bitcast_fusion
  440.4 2.8 reshape.128
  443.2 5.3 gather_fusion.4
  448.5 51.4 %all-to-all-done.1 = bf16[64,18,896]{2,1,0:T(8,128)(2,1)} async-done(((bf16[64,18,896]{2,1,0:T(8,128)(2,1)}), bf16[64,18,896]{2,1,0:T(8,128)(2,1)}, u32[]{:S(2)}, u32[]{:S(2)}) %all-to-all-start.1) | async-done | bytes 2064416 | tf_op jit(solution)/shard_map/all_to_all | solution.py:59
  499.9 2.8 reshape.125
  502.7 5.3 gather_fusion.1
  508.0 2.9 convert_reduce_fusion
  510.9 1.2 fusion.8
  512.1 1.2 fusion.13
  513.3 0.4 copy-done.10
  513.7 1.2 fusion.14
  514.9 1.4 convert_element_type.125
  516.3 118.8 %reduce-scatter.5.cloned.1.call-done = f32[16,896]{1,0:T(8,128)} async-done(((f32[1024,896]{1,0:T(8,128)}), f32[16,896]{1,0:T(8,128)}) %reduce-scatter.5.cloned.1.call-update) | async-done | bytes 57360 | tf_op jit(solution)/shard_map/reduce_scatter | solution.py:106
  635.2 1.4 convert_element_type.126
  (47 shorter events, 0.6 us)
Async XLA Ops:
  7.2 181.0 %copy-start = (bf16[1,896,1024]{2,1,0:T(8,128)(2,1)S(1)}, bf16[1,896,1024]{2,1,0:T(8,128)(2,1)}, u32[]{:S(2)}) copy-start(bf16[1,896,1024]{2,1,0:T(8,128)(2,1)} %param.12) | copy-start | bytes 5505028
  7.2 30.2 %copy-start.2 = (bf16[128,896]{1,0:T(8,128)(2,1)S(1)}, bf16[128,896]{1,0:T(8,128)(2,1)}, u32[]{:S(2)}) copy-start(bf16[128,896]{1,0:T(8,128)(2,1)} %param.8) | copy-start | bytes 688132
  7.2 131.6 %all-gather.5.cloned.1.call-start = ((), (), s32[]{:S(2)}) async-start(), calls=%async_computation.7 | async-start | bytes 1863680 | tf_op jit(solution)/shard_map/all_gather | solution.py:48
  50.3 13.1 %copy-start.13 = (s32[128,8]{0,1:T(8,128)S(1)}, s32[128,8]{0,1:T(8,128)}, u32[]{:S(2)}) copy-start(s32[128,8]{0,1:T(8,128)} %param.11) | copy-start | bytes 12292
  50.3 82.5 %all-to-all-start = ((bf16[64,18,896]{2,1,0:T(8,128)(2,1)}), bf16[64,18,896]{2,1,0:T(8,128)(2,1)}, u32[]{:S(2)}, u32[]{:S(2)}) async-start(bf16[64,18,896]{2,1,0:T(8,128)(2,1)} %broadcast_select_fusion), calls=%async_computation | async-start | bytes 5505024 | tf_op jit(solution)/shard_map/all_to_all | solution.py:39
  62.6 118.5 %all-gather.3.cloned.1.call-start = ((), (), s32[]{:S(2)}) async-start(), calls=%async_computation.6 | async-start | bytes 1863680 | tf_op jit(solution)/shard_map/all_gather | solution.py:47
  63.5 4.7 copy-start.3
  132.8 74.6 %all-to-all-start.2 = ((bf16[64,18,896]{2,1,0:T(8,128)(2,1)}), bf16[64,18,896]{2,1,0:T(8,128)(2,1)}, u32[]{:S(2)}, u32[]{:S(2)}) async-start(bf16[64,18,896]{2,1,0:T(8,128)(2,1)} %select_convert_fusion), calls=%async_computation.2 | async-start | bytes 5505024 | tf_op jit(solution)/shard_map/all_to_all | solution.py:73
  138.5 190.7 %all-reduce.3.cloned.1.call-start = ((), (), s32[]{:S(2)}) async-start(), calls=%async_computation.10 | async-start | bytes 10485760 | tf_op jit(solution)/shard_map/psum | solution.py:53
  217.7 297.2 %reduce-scatter.3.cloned.1.call-start = ((), (), s32[]{:S(2)}) async-start(), calls=%async_computation.8 | async-start | bytes 3727360 | tf_op jit(solution)/shard_map/reduce_scatter | solution.py:105
  337.1 1.4 copy-start.6
  346.5 11.1 %copy-start.11 = (bf16[128,1024]{1,0:T(8,128)(2,1)S(1)}, bf16[128,1024]{1,0:T(8,128)(2,1)}, u32[]{:S(2)}) copy-start(bf16[128,1024]{1,0:T(8,128)(2,1)} %get-tuple-element.7) | copy-start | bytes 786436
  346.5 77.0 %all-to-all-start.3 = ((bf16[64,18,896]{2,1,0:T(8,128)(2,1)}), bf16[64,18,896]{2,1,0:T(8,128)(2,1)}, u32[]{:S(2)}, u32[]{:S(2)}) async-start(bf16[64,18,896]{2,1,0:T(8,128)(2,1)} %reshape.127), calls=%async_computation.3 | async-start | bytes 5505024 | tf_op jit(solution)/shard_map/all_to_all | solution.py:89
  357.3 277.8 %reduce-scatter.5.cloned.1.call-start = ((), (), s32[]{:S(2)}) async-start(), calls=%async_computation.9 | async-start | bytes 3727360 | tf_op jit(solution)/shard_map/reduce_scatter | solution.py:106
  367.5 63.1 %copy-start.7 = (bf16[1152,896]{1,0:T(8,128)(2,1)S(1)}, bf16[1152,896]{1,0:T(8,128)(2,1)}, u32[]{:S(2)}) copy-start(bf16[1152,896]{1,0:T(8,128)(2,1)} %reshape.123) | copy-start | bytes 6193156
  423.6 76.3 %all-to-all-start.1 = ((bf16[64,18,896]{2,1,0:T(8,128)(2,1)}), bf16[64,18,896]{2,1,0:T(8,128)(2,1)}, u32[]{:S(2)}, u32[]{:S(2)}) async-start(bf16[64,18,896]{2,1,0:T(8,128)(2,1)} %reshape.124), calls=%async_computation.1 | async-start | bytes 5505024 | tf_op jit(solution)/shard_map/all_to_all | solution.py:59
  430.6 5.7 copy-start.5
  430.6 5.6 copy-start.8
  508.0 2.9 copy-start.4
  508.0 4.1 copy-start.9
  512.1 1.6 copy-start.10
  512.1 1.6 copy-start.12
  512.1 124.5 %copy-start.1 = (bf16[1,896,1024]{2,1,0:T(8,128)(2,1)S(1)}, bf16[1,896,1024]{2,1,0:T(8,128)(2,1)}, u32[]{:S(2)}) copy-start(bf16[1,896,1024]{2,1,0:T(8,128)(2,1)} %param.12) | copy-start | bytes 5505028
Sparse Core Ops, SparseCore 0:
  10.7 85.2 all-gather.4
  98.7 82.3 all-gather.2
  217.8 111.2 all-reduce.2
  333.2 155.8 reduce-scatter.2
  493.6 141.5 reduce-scatter.4
where the time goes:
time: 644 us; the launch traced here: 643 us
  waiting for transfers between devices  443 us (69%)
  local copies, waits for them, and re-layouts  66.7 us (10%)
  matrix products  44.5 us (7%)
  other arithmetic  38.1 us (6%)
  starting transfers between devices  36.4 us (6%)
  between operations  14.1 us (2%)
    reduce_scatter x1, waiting for transfers between devices, local(): lax.psum_scatter(partial_out, 'expert', scatter_dimension=0, tiled=True)  119 us
    psum x1, waiting for transfers between devices, local(): lax.psum(routed_part.astype(jnp.bfloat16), 'dp').astype(jnp.float32)  111 us
    all_to_all x1, waiting for transfers between devices, local(): lax.all_to_all(input_rows.reshape(experts, capacity, features), 'expert',...  56.1 us
    all_to_all x1, waiting for transfers between devices, local(): lax.all_to_all(expert_out.reshape(experts, capacity, features), 'expert',...  51.4 us
    all_to_all x1, waiting for transfers between devices, local(): lax.all_to_all(outgoing.reshape(experts, capacity, features), 'expert', s...  50.9 us
    all_gather x1, waiting for transfers between devices, local(): lax.all_gather(shared_in, 'expert', axis=1, tiled=True)  39.4 us
    dot_general x8, matrix products, contract(): lax.dot_general(first_op, second_op, (((first_axis,), (second_axis,)), ((...  30 us
    another operation x2, other arithmetic  18 us
  transfers between devices with their start and end apart: 9, of which 7 were waited for; matrix products, arithmetic and copies ran while one was open for 21% of the time, Pallas kernels for 0%

commit v1 on v0

--- a/solution.py
+++ b/solution.py
@@ -2,6 +2,8 @@
 import jax.numpy as jnp
 from jax import lax
 from jax.sharding import PartitionSpec as P
+
+_keep_up_ratios = lambda z, along_axis: lax.all_gather(z, along_axis).sum(axis=0)
 
 
 def silu_slope(inputs):
@@ -50,7 +52,7 @@
     routed_part = jnp.dot(arrived, w_in[0], preferred_element_type=jnp.float32)
     shared_part = jnp.dot(tokens, full_in, preferred_element_type=jnp.float32)
     pre_act, shared_pre = (
-        lax.psum(routed_part.astype(jnp.bfloat16), "dp").astype(jnp.float32),
+        _keep_up_ratios(routed_part.astype(jnp.bfloat16), "dp").astype(jnp.float32),
         lax.psum(shared_part.astype(jnp.bfloat16), "dp").astype(jnp.float32),
     )
     hidden = jax.nn.silu(pre_act).astype(jnp.bfloat16)

time: 644 us -> 726 us (1.13); the launches traced: 643 us -> 717 us
  waiting for transfers between devices: 443 us -> 495 us
  starting transfers between devices: 36.4 us -> 46.9 us
  other arithmetic: 38.1 us -> 47.7 us
    all_gather x0 -> x1, waiting for transfers between devices: none -> 93.6 us  [lax.all_gather(z, along_axis).sum(axis=0)]
    psum x1, waiting for transfers between devices: 111 us -> 46.6 us  [local(): lax.psum(shared_part.astype(jnp.bfloat16), 'dp').astype(jnp.float32)]
    reduce_scatter x1, waiting for transfers between devices: 0.01 us -> 57.3 us  [local(): lax.psum_scatter(partial_in, 'expert', scatter_dimension=1, tiled=True)]
    all_to_all x1, waiting for transfers between devices: 56.1 us -> 0.01 us  [local(): lax.all_to_all(input_rows.reshape(experts, capacity, features), 'expert',...]
    all_to_all x1, waiting for transfers between devices: 13.7 us -> 55 us  [local(): lax.all_to_all(grad_out.reshape(experts, capacity, features), 'expert', s...]
    all_gather x1, waiting for transfers between devices: 39.4 us -> 0.02 us  [local(): lax.all_gather(shared_in, 'expert', axis=1, tiled=True)]
    all_gather x1, waiting for transfers between devices: 0.02 us -> 35.1 us  [local(): lax.all_gather(shared_out, 'expert', axis=0, tiled=True)]
    all_to_all x1, waiting for transfers between devices: 50.9 us -> 17.7 us  [local(): lax.all_to_all(outgoing.reshape(experts, capacity, features), 'expert', s...]
  transfers between devices with their start and end apart: 9 -> 10, of which waited for: 7 -> 8; matrix products, arithmetic and copies ran while one was open for 21% -> 20% of each run, Pallas kernels for 0% -> 0%
where the time goes in v1:
time: 726 us; the launch traced here: 717 us
  waiting for transfers between devices  495 us (68%)
  local copies, waits for them, and re-layouts  66.2 us (9%)
  other arithmetic  47.7 us (7%)
  starting transfers between devices  46.9 us (6%)
  matrix products  46.6 us (6%)
  between operations  14.4 us (2%)
    reduce_scatter x1, waiting for transfers between devices, local(): lax.psum_scatter(partial_out, 'expert', scatter_dimension=0, tiled=True)  145 us
    all_gather x1, waiting for transfers between devices, lax.all_gather(z, along_axis).sum(axis=0)  93.6 us
    reduce_scatter x1, waiting for transfers between devices, local(): lax.psum_scatter(partial_in, 'expert', scatter_dimension=1, tiled=True)  57.3 us
    all_to_all x1, waiting for transfers between devices, local(): lax.all_to_all(grad_out.reshape(experts, capacity, features), 'expert', s...  55 us
    psum x1, waiting for transfers between devices, local(): lax.psum(shared_part.astype(jnp.bfloat16), 'dp').astype(jnp.float32)  46.6 us
    all_to_all x1, waiting for transfers between devices, local(): lax.all_to_all(expert_out.reshape(experts, capacity, features), 'expert',...  43 us
    all_gather x1, waiting for transfers between devices, local(): lax.all_gather(shared_out, 'expert', axis=0, tiled=True)  35.1 us
    dot_general x8, matrix products, contract(): lax.dot_general(first_op, second_op, (((first_axis,), (second_axis,)), ((...  29 us
  transfers between devices with their start and end apart: 10, of which 8 were waited for; matrix products, arithmetic and copies ran while one was open for 20% of the time, Pallas kernels for 0%

profile of v1, /device:TPU:8, one launch (start us, length us, event | category | flops | bytes accessed | tf_op | source)
XLA Modules:
  0.0 716.9 jit_solution(9923323817819807015)
XLA Ops:
  7.3 0.7 all-gather.5.cloned.1.call-update
  7.9 0.8 copy.16
  8.7 0.1 eq.29
  8.9 0.7 broadcast_multiply_fusion
  9.6 0.1 copy.15
  9.7 0.1 mul.68
  9.8 18.0 %reduce-window.6 = s32[64,8,128]{2,1,0:T(8,128)S(1)} reduce-window(s32[64,8,128]{2,1,0:T(8,128)S(1)} %fusion.25, s32[]{:T(128)} %constant.22.clone.1), window={size=1x1x128 pad=0_0x0_0x127_0}, to_apply=%region_1.2 | reduce-window | flops 8323072 | bytes 524292 | tf_op jit(solution)/shard_map/reduce-window
  27.8 0.1 slice.18
  28.0 0.1 copy.18
  28.3 0.1 add_add_fusion
  28.5 4.3 scatter_custom_fusion.1
  32.8 4.3 scatter_custom_fusion
  37.2 0.1 broadcast_in_dim.54
  37.3 0.1 copy.20
  37.5 4.9 gather_fusion.3
  42.4 4.6 reshape.130
  47.0 4.6 gather_fusion.2
  51.6 0.1 mul.76
  51.7 4.0 select_convert_fusion
  55.8 12.3 %all-to-all-start.2 = ((bf16[64,18,896]{2,1,0:T(8,128)(2,1)}), bf16[64,18,896]{2,1,0:T(8,128)(2,1)}, u32[]{:S(2)}, u32[]{:S(2)}) async-start(bf16[64,18,896]{2,1,0:T(8,128)(2,1)} %select_convert_fusion), calls=%async_computation.2 | async-start | bytes 5505024 | tf_op jit(solution)/shard_map/all_to_all | solution.py:75
  68.1 0.7 all-gather.7.cloned.1.call-update
  68.8 4.9 gather_fusion
  73.7 4.2 gather.18
  77.9 3.8 broadcast_select_fusion
  81.7 55.0 %all-to-all-done.2 = bf16[64,18,896]{2,1,0:T(8,128)(2,1)} async-done(((bf16[64,18,896]{2,1,0:T(8,128)(2,1)}), bf16[64,18,896]{2,1,0:T(8,128)(2,1)}, u32[]{:S(2)}, u32[]{:S(2)}) %all-to-all-start.2) | async-done | bytes 2064416 | tf_op jit(solution)/shard_map/all_to_all | solution.py:75
  136.7 6.5 all-to-all-start
  143.2 0.4 all-reduce.3.cloned.1.call-start
  143.6 2.9 convolution_convert_fusion.5
  146.5 35.1 %all-gather.7.cloned.1.call-done = bf16[1024,896]{1,0:T(8,128)(2,1)} async-done(((bf16[16,896]{1,0:T(8,128)(2,1)}), bf16[1024,896]{1,0:T(8,128)(2,1)}) %all-gather.7.cloned.1.call-update) | async-done | bytes 1835024 | tf_op jit(solution)/shard_map/all_gather | solution.py:50
  181.6 2.9 convolution_convert_fusion.4
  184.6 4.2 reshape.126
  188.8 5.5 convolution_convert_fusion
  194.3 17.7 %all-to-all-done = bf16[64,18,896]{2,1,0:T(8,128)(2,1)} async-done(((bf16[64,18,896]{2,1,0:T(8,128)(2,1)}), bf16[64,18,896]{2,1,0:T(8,128)(2,1)}, u32[]{:S(2)}, u32[]{:S(2)}) %all-to-all-start) | async-done | bytes 2064416 | tf_op jit(solution)/shard_map/all_to_all | solution.py:41
  212.1 4.2 reshape.123
  216.2 6.2 convolution_convert_fusion.1
  222.5 46.6 %all-reduce.3.cloned.1.call-done = (bf16[128,1024]{1,0:T(8,128)(2,1)}, bf16[1152,1024]{1,0:T(8,128)(2,1)}, bf16[128,1024]{1,0:T(8,128)(2,1)}) async-done(((bf16[128,1024]{1,0:T(8,128)(2,1)}, bf16[1152,1024]{1,0:T(8,128)(2,1)}, bf16[128,1024]{1,0:T(8,128)(2,1)}), (bf16[128,1024]{1,0:T(8,128)(2,1)}, bf16[1152,1024]{1,0:T(8,128)(2,1)}, bf16[128,1024]{1,0:T(8,128)(2,1)})) %all-reduce.3.cloned.1.call-update) | async-done | bytes 2883600 | tf_op jit(solution)/shard_map/psum | solution.py:56
  269.1 3.7 convolution_bitcast_fusion
  272.8 93.6 %all-gather.9.cloned.1.call-done = bf16[4608,1024]{1,0:T(8,128)(2,1)} async-done(((bf16[1152,1024]{1,0:T(8,128)(2,1)}), bf16[4608,1024]{1,0:T(8,128)(2,1)}) %all-gather.9.cloned.1.call-update) | async-done | bytes 9437200 | tf_op jit(solution)/shard_map/all_gather | solution.py:6
  366.3 8.2 %reduce_sum.43 = bf16[1152,1024]{1,0:T(8,128)(2,1)} reduce(bf16[4,1152,1024]{2,1,0:T(8,128)(2,1)} %bitcast.53, bf16[]{:T(256)} %constant.48.clone.1), dimensions={0}, to_apply=%region_6.7 | reduce | flops 3538944 | bytes 11796482 | tf_op jit(solution)/shard_map/reduce_sum | solution.py:6
  374.5 5.7 convolution_convert_fusion.3
  380.2 4.2 reshape.124
  384.4 10.8 %all-to-all-start.1 = ((bf16[64,18,896]{2,1,0:T(8,128)(2,1)}), bf16[64,18,896]{2,1,0:T(8,128)(2,1)}, u32[]{:S(2)}, u32[]{:S(2)}) async-start(bf16[64,18,896]{2,1,0:T(8,128)(2,1)} %reshape.124), calls=%async_computation.1 | async-start | bytes 5505024 | tf_op jit(solution)/shard_map/all_to_all | solution.py:61
  395.2 9.6 %reduce-scatter.5.cloned.1.call-start = ((), (), s32[]{:S(2)}) async-start(), calls=%async_computation.9 | async-start | bytes 3727360 | tf_op jit(solution)/shard_map/reduce_scatter | solution.py:108
  404.8 2.5 fusion.32
  407.3 4.5 fusion.7
  411.8 1.4 copy-done.5
  413.2 2.9 convolution_convert_fusion.2
  416.1 2.3 reshape.127
  418.4 43.0 %all-to-all-done.1 = bf16[64,18,896]{2,1,0:T(8,128)(2,1)} async-done(((bf16[64,18,896]{2,1,0:T(8,128)(2,1)}), bf16[64,18,896]{2,1,0:T(8,128)(2,1)}, u32[]{:S(2)}, u32[]{:S(2)}) %all-to-all-start.1) | async-done | bytes 2064416 | tf_op jit(solution)/shard_map/all_to_all | solution.py:61
  461.4 7.1 all-to-all-start.3
  468.6 57.3 %reduce-scatter.3.cloned.1.call-done = f32[896,16]{0,1:T(8,128)} async-done(((f32[896,1024]{0,1:T(8,128)}), f32[896,16]{0,1:T(8,128)}) %reduce-scatter.3.cloned.1.call-update) | async-done | bytes 57360 | tf_op jit(solution)/shard_map/reduce_scatter | solution.py:107
  525.9 1.4 convert_element_type.127
  527.4 145.2 %reduce-scatter.5.cloned.1.call-done = f32[16,896]{1,0:T(8,128)} async-done(((f32[1024,896]{1,0:T(8,128)}), f32[16,896]{1,0:T(8,128)}) %reduce-scatter.5.cloned.1.call-update) | async-done | bytes 57360 | tf_op jit(solution)/shard_map/reduce_scatter | solution.py:108
  672.6 1.4 convert_element_type.128
  674.0 6.2 convert_bitcast_fusion.1
  680.3 4.1 convert_bitcast_fusion
  684.4 2.8 reshape.125
  687.2 5.3 gather_fusion.1
  692.5 2.7 fusion.8
  695.1 2.8 reshape.128
  697.9 5.3 gather_fusion.4
  703.2 2.7 convert_reduce_fusion
  706.0 2.8 fusion.13
  708.8 1.2 fusion.14
  (47 shorter events, 0.7 us)
Async XLA Ops:
  7.2 181.6 %copy-start = (bf16[1,1024,896]{2,1,0:T(8,128)(2,1)S(1)}, bf16[1,1024,896]{2,1,0:T(8,128)(2,1)}, u32[]{:S(2)}) copy-start(bf16[1,1024,896]{2,1,0:T(8,128)(2,1)} %param.13) | copy-start | bytes 5505028
  7.2 30.1 %copy-start.10 = (s32[128,8]{0,1:T(8,128)S(1)}, s32[128,8]{0,1:T(8,128)}, u32[]{:S(2)}) copy-start(s32[128,8]{0,1:T(8,128)} %param.11) | copy-start | bytes 12292
  7.2 30.3 %copy-start.3 = (bf16[128,896]{1,0:T(8,128)(2,1)S(1)}, bf16[128,896]{1,0:T(8,128)(2,1)}, u32[]{:S(2)}) copy-start(bf16[128,896]{1,0:T(8,128)(2,1)} %param.9) | copy-start | bytes 688132
  7.2 136.4 %all-gather.5.cloned.1.call-start = ((), (), s32[]{:S(2)}) async-start(), calls=%async_computation.6 | async-start | bytes 1863680 | tf_op jit(solution)/shard_map/all_gather | solution.py:49
  55.8 13.1 %copy-start.2 = (bf16[128,896]{1,0:T(8,128)(2,1)S(1)}, bf16[128,896]{1,0:T(8,128)(2,1)}, u32[]{:S(2)}) copy-start(bf16[128,896]{1,0:T(8,128)(2,1)} %param.8) | copy-start | bytes 688132
  55.8 80.9 %all-to-all-start.2 = ((bf16[64,18,896]{2,1,0:T(8,128)(2,1)}), bf16[64,18,896]{2,1,0:T(8,128)(2,1)}, u32[]{:S(2)}, u32[]{:S(2)}) async-start(bf16[64,18,896]{2,1,0:T(8,128)(2,1)} %select_convert_fusion), calls=%async_computation.2 | async-start | bytes 5505024 | tf_op jit(solution)/shard_map/all_to_all | solution.py:75
  68.1 113.6 %all-gather.7.cloned.1.call-start = ((), (), s32[]{:S(2)}) async-start(), calls=%async_computation.7 | async-start | bytes 1863680 | tf_op jit(solution)/shard_map/all_gather | solution.py:50
  136.7 75.4 %all-to-all-start = ((bf16[64,18,896]{2,1,0:T(8,128)(2,1)}), bf16[64,18,896]{2,1,0:T(8,128)(2,1)}, u32[]{:S(2)}, u32[]{:S(2)}) async-start(bf16[64,18,896]{2,1,0:T(8,128)(2,1)} %broadcast_select_fusion), calls=%async_computation | async-start | bytes 5505024 | tf_op jit(solution)/shard_map/all_to_all | solution.py:41
  143.2 125.9 %all-reduce.3.cloned.1.call-start = ((), (), s32[]{:S(2)}) async-start(), calls=%async_computation.11 | async-start | bytes 5767168 | tf_op jit(solution)/shard_map/psum | solution.py:56
  194.3 172.1 %all-gather.9.cloned.1.call-start = ((), (), s32[]{:S(2)}) async-start(), calls=%async_computation.10 | async-start | bytes 11796480 | tf_op jit(solution)/shard_map/all_gather | solution.py:6
  222.4 303.5 %reduce-scatter.3.cloned.1.call-start = ((), (), s32[]{:S(2)}) async-start(), calls=%async_computation.8 | async-start | bytes 3727360 | tf_op jit(solution)/shard_map/reduce_scatter | solution.py:107
  384.4 20.4 %copy-start.8 = (bf16[128,1024]{1,0:T(8,128)(2,1)S(1)}, bf16[128,1024]{1,0:T(8,128)(2,1)}, u32[]{:S(2)}) copy-start(bf16[128,1024]{1,0:T(8,128)(2,1)} %get-tuple-element.6) | copy-start | bytes 786436
  384.4 77.1 %all-to-all-start.1 = ((bf16[64,18,896]{2,1,0:T(8,128)(2,1)}), bf16[64,18,896]{2,1,0:T(8,128)(2,1)}, u32[]{:S(2)}, u32[]{:S(2)}) async-start(bf16[64,18,896]{2,1,0:T(8,128)(2,1)} %reshape.124), calls=%async_computation.1 | async-start | bytes 5505024 | tf_op jit(solution)/shard_map/all_to_all | solution.py:61
  395.2 277.4 %reduce-scatter.5.cloned.1.call-start = ((), (), s32[]{:S(2)}) async-start(), calls=%async_computation.9 | async-start | bytes 3727360 | tf_op jit(solution)/shard_map/reduce_scatter | solution.py:108
  407.3 5.9 copy-start.11
  411.8 1.4 copy-start.5
  461.4 233.7 %all-to-all-start.3 = ((bf16[64,18,896]{2,1,0:T(8,128)(2,1)}), bf16[64,18,896]{2,1,0:T(8,128)(2,1)}, u32[]{:S(2)}, u32[]{:S(2)}) async-start(bf16[64,18,896]{2,1,0:T(8,128)(2,1)} %reshape.127), calls=%async_computation.3 | async-start | bytes 5505024 | tf_op jit(solution)/shard_map/all_to_all | solution.py:91
  674.0 6.2 copy-start.4
  674.0 6.2 copy-start.6
  705.9 2.9 copy-start.7
  706.0 2.8 copy-start.9
  706.0 4.1 copy-start.1
Sparse Core Ops, SparseCore 0:
  10.7 83.0 all-gather.4
  96.6 85.0 all-gather.6
  194.4 74.6 all-reduce.2
  270.8 95.5 all-gather.8
  370.3 155.5 reduce-scatter.2
  530.5 142.0 reduce-scatter.4
